TPU v7x, 32 devices: a whole 2x2x4 slice. The times are simulated.
32 devices in a mesh: replica: 8 (over z, x), brick: 4 (over y, core).
Axes of the slice: x: 2, y: 2, z: 4, core: 2. Of those that a mesh axis runs over, the one named last changes fastest.
Arguments:
- atom_locations: float32 [8, 3, 3072], P('replica', None, 'brick'), may hold values from 0 to 128, as said below
- atom_speeds_vector: float32 [8, 3, 3072], P('replica', None, 'brick'), may hold values from -7 to 7
- inertial_amounts: float32 [3072], P('brick'), may hold values from 1 to 4
- electric_loads: float32 [3072], P('brick'), may hold values from -4 to 4
- scatter_strengths: float32 [3072], P('brick'), may hold values from 0.5 to 2
- gaussian_spreads_sigma: float32 [3072], P('brick'), may hold values from 0.7 to 1.4
- atom_present_flags: int32 [3072], P('brick'), may hold values 0 or 1
- observed_volume_values: float32 [40, 128, 128], P('brick'), may hold values from 0 to 2
- voxel_reciprocal_spread: float32 [40, 128, 128], P('brick'), may hold values from 0.5 to 4
- paired_partner_lists: int32 [24, 14], P('brick'), may hold values from 0 to 9
- cell_usage_tally: int32 [24], P('brick'), may hold values from 1 to 14, as said below
- halo_sender_spots: int32 [2, 1024], P(None, 'brick'), may hold values from 0 to 767
- target_warmth_levels: int32 [8], P('replica'), may hold values from 280 to 399
Outputs:
- new_positions: float32 [8, 3, 3072], P('replica', None, 'brick')
- new_velocities: float32 [8, 3, 3072], P('replica', None, 'brick')
- deviation: float32 [40, 128, 128], P('brick', 'replica')
Inputs may be any that keep to these rules, and one draw needn't show every extreme that they name: `atom_locations`: atoms in the slots of brick b have x in [b * 10, (b + 1) * 10), y in [0, 128), z in [0, 128). Only the first cell_usage_tally[c] slots of cell c count; some cell uses all 14 slots.
All inputs are finite; a program needn't handle non-finite values. No bound on the sum of `atom_present_flags` on one device may be relied on, other than what follows from the above.
Results may differ from a plain program's by a relative error of at most 0.00062.
Values may be sent and summed in bfloat16 or wider, within the bound.
No kernel may reach another device: no remote copies, remote signals or barrier semaphores. Data moves between devices by JAX's collectives and lax.ppermute only.
A program may use at most 64 MiB of HBM per device.

v0:
```python
import jax
import jax.numpy as jnp
from jax import lax
from jax.sharding import PartitionSpec as P

HALO = 2
CELL = 128


restraint = 0.1
coupling = 5.0
softening = 1.0
timestep = 0.5
boltzmann = 0.015
heat_bath_damping = 0.5


def from_behind(block, axis, distance):
    devices = range(lax.axis_size(axis))
    route = [((i - distance) % len(devices), i) for i in devices]
    return lax.ppermute(block, axis, route)


def padded(block, sides, width):
    for axis, dim in sides:
        count = lax.axis_size(axis)
        forward = [(i, i + 1) for i in range(count - 1)]
        forward.append((count - 1, 0))
        backward = [(target, source) for source, target in forward]
        low = lax.ppermute(
            lax.slice_in_dim(block, block.shape[dim] - width, None, axis=dim), axis, forward
        )
        high = lax.ppermute(lax.slice_in_dim(block, 0, width, axis=dim), axis, backward)
        block = jnp.concatenate([low, block, high], axis=dim)
    return block


def wrapped(delta, period):
    return delta - period * jnp.floor(delta / period + 0.5)


def factors(grid, coord, inv_var, period):
    delta = wrapped(grid[:, None] - coord[None, :], period)
    value = jnp.exp(-0.5 * delta * delta * inv_var[None, :])
    return (value, delta * inv_var[None, :] * value)


def spread(x_val, y_val, z_fac, amp):

    def spread_one_plane(row):
        left = ((amp * row)[None, :] * y_val).astype(jnp.bfloat16)
        return lax.dot_general(
            left, z_fac, (((1,), (1,)), ((), ())), preferred_element_type=jnp.float32
        )

    return lax.map(spread_one_plane, x_val)


def map_forces(grad_ext, x_val, x_der, y_val, y_der, z_pair, amp):
    count = amp.shape[0]

    def map_one_plane(carry, inputs):
        plane, x_one, x_slope = inputs
        product = jnp.dot(plane, z_pair, preferred_element_type=jnp.float32)
        along = product[:, :count]
        across = product[:, count:]
        first = jnp.sum(y_val * along, axis=0)
        second = jnp.sum(y_der * along, axis=0)
        third = jnp.sum(y_val * across, axis=0)
        return (carry + jnp.stack([x_slope * first, x_one * second, x_one * third]), None)

    total, _ = lax.scan(map_one_plane, jnp.zeros((3, count), jnp.float32), (grad_ext, x_val, x_der))
    return -amp[None, :] * total


def pair_forces(coords, charge, ghost_low, ghost_high, paired_partner_lists, live, periods, limit):
    own = jnp.concatenate([coords, charge[None, :]], 0).reshape(4, -1, CELL)
    blocks = jnp.concatenate(
        [own, ghost_low.reshape(4, -1, CELL), ghost_high.reshape(4, -1, CELL)], axis=1
    )
    period = jnp.array([float(p) for p in periods], jnp.float32)[:, None, None, None]

    def slot(index, total):
        partner = jnp.take(blocks, paired_partner_lists[:, index], axis=1)
        delta = wrapped(own[:3, :, :, None] - partner[:3, :, None, :], period)
        dist = jnp.sum(delta * delta, axis=0) + softening
        active = (index < live).astype(jnp.float32)
        scale = (
            coupling
            * own[3][:, :, None]
            * partner[3][:, None, :]
            * active[:, None, None]
            / (dist * jnp.sqrt(dist))
        )
        return total + jnp.sum(scale[None] * delta, axis=3)

    total = lax.fori_loop(0, limit, slot, jnp.zeros((3, own.shape[1], CELL), jnp.float32))
    return total.reshape(3, -1)


def local(
    atom_locations,
    atom_speeds_vector,
    inertial_amounts,
    electric_loads,
    scatter_strengths,
    gaussian_spreads_sigma,
    atom_present_flags,
    observed_volume_values,
    voxel_reciprocal_spread,
    paired_partner_lists,
    cell_usage_tally,
    halo_sender_spots,
    target_warmth_levels,
):
    thick, rows, depth = observed_volume_values.shape
    slabs = lax.axis_size("brick")
    members = lax.axis_size("replica")
    brick = lax.axis_index("brick")
    n_x = thick * slabs
    coords = atom_locations[0]
    count = coords.shape[1]
    occupancy = atom_present_flags.astype(jnp.float32)
    amp = occupancy * scatter_strengths
    charge = occupancy * electric_loads
    inv_var = 1.0 / (gaussian_spreads_sigma * gaussian_spreads_sigma)
    planes = thick + 2 * HALO
    plane_grid = (brick * thick - HALO + jnp.arange(planes, dtype=jnp.int32)).astype(jnp.float32)
    x_val, x_der = factors(plane_grid, coords[0], inv_var, n_x)
    y_val, y_der = factors(
        jnp.arange(rows, dtype=jnp.int32).astype(jnp.float32), coords[1], inv_var, rows
    )
    z_val, z_der = factors(
        jnp.arange(depth, dtype=jnp.int32).astype(jnp.float32), coords[2], inv_var, depth
    )
    z_pair = jnp.concatenate([z_val, z_der], axis=1).astype(jnp.bfloat16)
    partial_value = spread(x_val, y_val, z_pair[:, :count], amp)
    packet_up = jnp.concatenate(
        [
            jnp.take(coords, halo_sender_spots[0], axis=1),
            jnp.take(charge, halo_sender_spots[0])[None, :],
        ],
        0,
    )
    packet_down = jnp.concatenate(
        [
            jnp.take(coords, halo_sender_spots[1], axis=1),
            jnp.take(charge, halo_sender_spots[1])[None, :],
        ],
        0,
    )
    rim_low, ghost_low = from_behind((partial_value[thick + HALO :], packet_up), "brick", 1)
    rim_high, ghost_high = from_behind((partial_value[:HALO], packet_down), "brick", -1)
    pad_low = jnp.pad(rim_low, ((0, thick - HALO), (0, 0), (0, 0)))
    pad_high = jnp.pad(rim_high, ((thick - HALO, 0), (0, 0), (0, 0)))
    local_map = partial_value[HALO : HALO + thick] + pad_low + pad_high
    share_rows = rows // members
    start = lax.axis_index("replica") * share_rows
    summed = lax.psum(local_map, "replica")
    whole = summed / members - observed_volume_values
    grad = (restraint * voxel_reciprocal_spread * whole).astype(jnp.bfloat16)
    deviation = lax.dynamic_slice_in_dim(whole, start, share_rows, 1)
    grad_ext = padded(grad, (("brick", 0),), HALO)
    restraint_force = map_forces(grad_ext, x_val, x_der, y_val, y_der, z_pair, amp)
    limit = paired_partner_lists.shape[1]
    short = pair_forces(
        coords,
        charge,
        ghost_low,
        ghost_high,
        paired_partner_lists,
        cell_usage_tally,
        (n_x, rows, depth),
        limit,
    )
    forces = restraint_force + short
    v_half = atom_speeds_vector[0] + timestep * forces / inertial_amounts[None, :]
    kinetic = lax.psum(jnp.sum(inertial_amounts[None, :] * v_half * v_half), "brick")
    present_moment = kinetic / (3 * count * slabs * boltzmann) + 1e-06
    rescale_ratio = jnp.sqrt(
        1.0
        + heat_bath_damping * (target_warmth_levels[0].astype(jnp.float32) / present_moment - 1.0)
    )
    new_velocities = rescale_ratio * v_half
    new_positions = coords + timestep * new_velocities
    return (new_positions[None], new_velocities[None], deviation)


def solution(mesh):
    return jax.shard_map(
        local,
        mesh=mesh,
        in_specs=(
            P("replica", None, "brick"),
            P("replica", None, "brick"),
            P("brick"),
            P("brick"),
            P("brick"),
            P("brick"),
            P("brick"),
            P("brick", None, None),
            P("brick", None, None),
            P("brick", None),
            P("brick"),
            P(None, "brick"),
            P("replica"),
        ),
        out_specs=(
            P("replica", None, "brick"),
            P("replica", None, "brick"),
            P("brick", "replica", None),
        ),
        check_vma=False,
    )
```

profile of v0, /device:TPU:0, one launch (start us, length us, event | category | flops | bytes accessed | tf_op | source)
XLA Modules:
  0.0 137.5 jit_solution(13202782930005128949)
XLA Ops:
  7.2 0.8 fusion.82
  8.0 0.7 copy.92
  8.7 0.7 fusion.79
  9.4 1.4 gather_fusion.4
  11.0 0.7 gather_fusion.3
  11.9 2.5 %collective-permute-start.5 = (f32[4,256]{1,0:T(4,128)S(1)}, f32[4,256]{1,0:T(4,128)S(1)}, u32[]{:S(2)}, u32[]{:S(2)}) collective-permute-start(f32[4,256]{1,0:T(4,128)S(1)} %pad_maximum_fusion.5), channel_id=1, source_target_pairs={{1,0},{2,1},{3,2},{0,3},{5,4},{6,5},{7,6},{4,7},{9,8},{10,9},{11,1... | collective-permute-start | bytes 12296 | tf_op jit(solution)/shard_map/ppermute | solution.py:21
  14.4 1.4 gather_fusion.2
  15.8 0.7 gather_fusion.1
  17.0 7.7 %while.40 = (s32[]{:T(128)}, f32[14,128,128]{2,1,0:T(8,128)S(1)}, f32[768]{0:T(1024)S(1)}, f32[14,768]{1,0:T(8,128)S(1)}, f32[768]{0:T(1024)S(1)}, /*index=5*/f3...) while((s32[]{:T(128)}, f32[14,128,128]{2,1,0:T(8,128)S(1)}, ...), condition=%wide.region_1.2_spmd.clone.clone, body=%wide.region_0.1_spmd.clone.clone.sunk | while | flops 27230976 | bytes 96365 | solution.py:56
  24.8 0.7 collective-permute-start
  25.5 1.1 collective-permute-start.1
  27.8 1.5 %collective-permute-done = f32[2,128,128]{2,1,0:T(8,128)S(1)} collective-permute-done((f32[2,128,128]{2,1,0:T(8,128)S(1)}, f32[2,128,128]{2,1,0:T(8,128)S(1)}, u32[]{:S(2)}, u32[]{:S(2)}) %collective-permute-start) | collective-permute-done | bytes 131104 | tf_op jit(solution)/shard_map/ppermute | solution.py:21
  29.3 0.9 pad_add_fusion
  30.3 29.7 %while.41 = (s32[]{:T(128)}, f32[3,6,128]{2,1,0:T(8,128)S(1)}, f32[4,6,128]{2,1,0:T(8,128)S(1)}, s32[6,14]{0,1:T(8,128)S(1)}, f32[4,10,128]{2,0,1:T(4,128)S(1)},...) while((s32[]{:T(128)}, f32[3,6,128]{2,1,0:T(8,128)S(1)}, ...), condition=%wide.region_11.14_spmd.clone.clone, body=%wide.region_8.13_spmd.clone.clone.sunk | while | flops 5119027 | bytes 1761635 | solution.py:97
  30.4 0.6 gather_fusion
  31.7 0.7 fusion.98
  32.5 0.6 gather_fusion
  33.8 0.7 fusion.98
  34.6 0.6 gather_fusion
  35.9 0.7 fusion.98
  36.7 0.6 gather_fusion
  38.0 0.7 fusion.98
  38.8 0.6 gather_fusion
  40.1 0.7 fusion.98
  41.0 0.6 gather_fusion
  42.3 0.7 fusion.98
  43.1 0.6 gather_fusion
  44.4 0.7 fusion.98
  45.2 0.6 gather_fusion
  46.5 0.7 fusion.98
  47.3 0.6 gather_fusion
  48.6 0.7 fusion.98
  49.4 0.6 gather_fusion
  50.7 0.7 fusion.98
  52.9 0.7 fusion.98
  55.0 0.7 fusion.98
  57.1 0.7 fusion.98
  59.2 0.7 fusion.98
  60.0 45.7 %all-reduce.4.cloned.1.call-done = f32[10,128,128]{2,1,0:T(8,128)} async-done(((f32[10,128,128]{2,1,0:T(8,128)}), f32[10,128,128]{2,1,0:T(8,128)}) %all-reduce.4.cloned.1.call-update) | async-done | bytes 655376 | tf_op jit(solution)/shard_map/psum | solution.py:159
  105.7 1.3 multiply_convert_fusion
  107.0 1.7 %collective-permute-start.3 = (bf16[2,128,128]{2,1,0:T(8,128)(2,1)S(1)}, bf16[2,128,128]{2,1,0:T(8,128)(2,1)S(1)}, u32[]{:S(2)}, u32[]{:S(2)}) collective-permute-start(bf16[2,128,128]{2,1,0:T(8,128)(2,1)S(1)} %get-tuple-element.542), channel_id=1, source_target_pairs={{1,0},{2,1},{3,2},{0,3},{5,4},{6,5},{7,6},{4,7},{9,8},{10,9},{11,1... | collective-permute-start | bytes 196616 | tf_op jit(solution)/shard_map/ppermute | solution.py:33
  108.8 0.6 constant_dynamic-slice_fusion
  109.4 1.3 collective-permute-done.2
  110.8 9.2 %while.42 = (s32[]{:T(128)}, f32[3,768]{1,0:T(4,128)S(1)}, f32[14,768]{1,0:T(8,128)S(1)}, bf16[14,128,128]{2,1,0:T(8,128)(2,1)S(1)}, bf16[128,1536]{1,0:T(8,128)...) while((s32[]{:T(128)}, f32[3,768]{1,0:T(4,128)S(1)}, ...), condition=%wide.region_7.8_spmd.clone.clone.clone, body=%wide.region_3.7_spmd.clone.clone.clone.sunk | while | flops 52012032 | bytes 2067079 | solution.py:72
  120.0 0.6 fusion.77
  120.6 8.0 %psum.15 = f32[]{:T(128)} all-reduce(f32[]{:T(128)} %get-tuple-element.524), channel_id=1, replica_groups=mesh['replica'=8,'brick'=4] {'brick'}, use_global_device_ids=true, to_apply=%region_13.16 | all-reduce | flops 1 | bytes 8 | tf_op jit(solution)/shard_map/psum | solution.py:178
  129.4 0.6 copy.79
  130.0 0.6 copy.78
  (300 shorter events, 29.8 us)
Async XLA Ops:
  7.2 98.5 %all-reduce.4.cloned.1.call-start = ((), (), s32[]{:S(2)}) async-start(), calls=%async_computation | async-start | bytes 1310720 | tf_op jit(solution)/shard_map/psum | solution.py:159
  11.7 5.1 %copy-start.2 = (f32[1,3,768]{2,0,1:T(1,128)S(1)}, f32[1,3,768]{2,0,1:T(1,128)}, u32[]{:S(2)}) copy-start(f32[1,3,768]{2,0,1:T(1,128)} %param.24) | copy-start | bytes 27652
  11.9 15.8 %collective-permute-start.5 = (f32[4,256]{1,0:T(4,128)S(1)}, f32[4,256]{1,0:T(4,128)S(1)}, u32[]{:S(2)}, u32[]{:S(2)}) collective-permute-start(f32[4,256]{1,0:T(4,128)S(1)} %pad_maximum_fusion.5), channel_id=1, source_target_pairs={{1,0},{2,1},{3,2},{0,3},{5,4},{6,5},{7,6},{4,7},{9,8},{10,9},{11,1... | collective-permute-start | bytes 12296 | tf_op jit(solution)/shard_map/ppermute | solution.py:21
  16.8 11.0 %collective-permute-start.4 = (f32[4,256]{1,0:T(4,128)S(1)}, f32[4,256]{1,0:T(4,128)S(1)}, u32[]{:S(2)}, u32[]{:S(2)}) collective-permute-start(f32[4,256]{1,0:T(4,128)S(1)} %pad_maximum_fusion.4), channel_id=1, source_target_pairs={{3,0},{0,1},{1,2},{2,3},{7,4},{4,5},{5,6},{6,7},{11,8},{8,9},{9,10... | collective-permute-start | bytes 12296 | tf_op jit(solution)/shard_map/ppermute | solution.py:21
  24.7 2.9 %copy-start.6 = (s32[6,14]{1,0:T(8,128)S(1)}, s32[6,14]{1,0:T(8,128)}, u32[]{:S(2)}) copy-start(s32[6,14]{1,0:T(8,128)} %param.33) | copy-start | bytes 1012
  24.8 4.5 %collective-permute-start = (f32[2,128,128]{2,1,0:T(8,128)S(1)}, f32[2,128,128]{2,1,0:T(8,128)S(1)}, u32[]{:S(2)}, u32[]{:S(2)}) collective-permute-start(f32[2,128,128]{2,1,0:T(8,128)S(1)} %get-tuple-element.539), channel_id=1, source_target_pairs={{3,0},{0,1},{1,2},{2,3},{7,4},{4,5},{5,6},{6,7},{11,8},{8,9},{9,10... | collective-permute-start | bytes 393224 | tf_op jit(solution)/shard_map/ppermute | solution.py:21
  25.5 3.8 %collective-permute-start.1 = (f32[2,128,128]{2,1,0:T(8,128)S(1)}, f32[2,128,128]{2,1,0:T(8,128)S(1)}, u32[]{:S(2)}, u32[]{:S(2)}) collective-permute-start(f32[2,128,128]{2,1,0:T(8,128)S(1)} %get-tuple-element.540), channel_id=1, source_target_pairs={{1,0},{2,1},{3,2},{0,3},{5,4},{6,5},{7,6},{4,7},{9,8},{10,9},{11,1... | collective-permute-start | bytes 393224 | tf_op jit(solution)/shard_map/ppermute | solution.py:21
  27.8 2.5 %copy-start.3 = (f32[3]{0:T(128)S(1)}, f32[3]{0:T(128)}, u32[]{:S(2)}) copy-start(f32[3]{0:T(128)} %constant.342) | copy-start | bytes 40
  27.8 2.5 %copy-start.4 = (f32[3]{0:T(128)S(1)}, f32[3]{0:T(128)}, u32[]{:S(2)}) copy-start(f32[3]{0:T(128)} %constant.341) | copy-start | bytes 40
  27.8 2.5 %copy-start.8 = (s32[6]{0:T(128)S(1)}, s32[6]{0:T(128)}, u32[]{:S(2)}) copy-start(s32[6]{0:T(128)} %param.34) | copy-start | bytes 76
  30.3 75.4 %copy-start = (f32[10,128,128]{2,1,0:T(8,128)S(1)}, f32[10,128,128]{2,1,0:T(8,128)}, u32[]{:S(2)}) copy-start(f32[10,128,128]{2,1,0:T(8,128)} %param.32) | copy-start | bytes 1966084
  30.3 75.4 %copy-start.1 = (f32[10,128,128]{2,1,0:T(8,128)S(1)}, f32[10,128,128]{2,1,0:T(8,128)}, u32[]{:S(2)}) copy-start(f32[10,128,128]{2,1,0:T(8,128)} %param.31) | copy-start | bytes 1966084
  107.0 3.7 %collective-permute-start.2 = (bf16[2,128,128]{2,1,0:T(8,128)(2,1)S(1)}, bf16[2,128,128]{2,1,0:T(8,128)(2,1)S(1)}, u32[]{:S(2)}, u32[]{:S(2)}) collective-permute-start(bf16[2,128,128]{2,1,0:T(8,128)(2,1)S(1)} %get-tuple-element.541), channel_id=1, source_target_pairs={{0,1},{1,2},{2,3},{3,0},{4,5},{5,6},{6,7},{7,4},{8,9},{9,10},{10,1... | collective-permute-start | bytes 196616 | tf_op jit(solution)/shard_map/ppermute | solution.py:30
  107.0 3.7 %collective-permute-start.3 = (bf16[2,128,128]{2,1,0:T(8,128)(2,1)S(1)}, bf16[2,128,128]{2,1,0:T(8,128)(2,1)S(1)}, u32[]{:S(2)}, u32[]{:S(2)}) collective-permute-start(bf16[2,128,128]{2,1,0:T(8,128)(2,1)S(1)} %get-tuple-element.542), channel_id=1, source_target_pairs={{1,0},{2,1},{3,2},{0,3},{5,4},{6,5},{7,6},{4,7},{9,8},{10,9},{11,1... | collective-permute-start | bytes 196616 | tf_op jit(solution)/shard_map/ppermute | solution.py:33
  110.8 9.2 %copy-start.5 = (f32[1,3,768]{2,0,1:T(1,128)S(1)}, f32[1,3,768]{2,0,1:T(1,128)}, u32[]{:S(2)}) copy-start(f32[1,3,768]{2,0,1:T(1,128)} %param.25) | copy-start | bytes 27652
  110.8 9.2 %copy-start.7 = (f32[768]{0:T(1024)S(1)}, f32[768]{0:T(1024)}, u32[]{:S(2)}) copy-start(f32[768]{0:T(1024)} %param.26) | copy-start | bytes 9220
Sparse Core Ops, SparseCore 0:
  30.4 75.2 all-reduce.3
where the time goes:
time: 138 us; the launch traced here: 137 us
  waiting for transfers between devices  48.5 us (35%)
  other arithmetic  30 us (22%)
  local copies, waits for them, and re-layouts  16.3 us (12%)
  between operations  15.8 us (11%)
  matrix products  10.4 us (8%)
  blocking collectives  8 us (6%)
  starting transfers between devices  6.2 us (4%)
  loops' own time  2.32 us (2%)
    psum x1, waiting for transfers between devices, local(): summed = lax.psum(local_map, 'replica')  45.7 us
    reduce_sum x14, other arithmetic, slot(): return total + jnp.sum(scale[None] * delta, axis=3)  10.2 us
    gather x14, local copies, waits for them, and re-layouts, slot(): partner = jnp.take(blocks, paired_partner_lists[:, index], axis=1)  8.02 us
    psum x1, blocking collectives, local(): lax.psum(jnp.sum(inertial_amounts[None, :] * v_half * v_half), 'brick')  8 us
    dot_general x14, matrix products, spread_one_plane(): lax.dot_general(left, z_fac, (((1,), (1,)), ((), ())), preferred_element_...  7.01 us
    reduce_sum x14, other arithmetic, slot(): dist = jnp.sum(delta * delta, axis=0) + softening  5.37 us
    reduce_sum x14, other arithmetic, map_one_plane(): first = jnp.sum(y_val * along, axis=0)  4.58 us
    ppermute x4, starting transfers between devices, from_behind(): return lax.ppermute(block, axis, route)  4.37 us
  transfers between devices with their start and end apart: 7, of which 3 were waited for; matrix products, arithmetic and copies ran while one was open for 28% of the time, Pallas kernels for 0%

commit v1 on v0

v1 whole, which is shorter than its diff:
```python
import functools

import jax
import jax.numpy as jnp
from jax import lax
from jax.experimental import pallas as pl
from jax.experimental.pallas import tpu as pltpu
from jax.sharding import PartitionSpec as P

HALO = 2
CELL = 128
RIM = 2 * HALO

restraint = 0.1
coupling = 5.0
softening = 1.0
timestep = 0.5
boltzmann = 0.015
heat_bath_damping = 0.5

F32 = jnp.float32
BF16 = jnp.bfloat16
NT = (((1,), (1,)), ((), ()))
VMEM = pl.BlockSpec(memory_space=pltpu.VMEM)
SMEM = pl.BlockSpec(memory_space=pltpu.SMEM)
ANY = pl.BlockSpec(memory_space=pl.ANY)


def wrapped(delta, period):
    return delta - period * jnp.floor(delta / period + 0.5)


def gauss(grid, coord, inv_var, period):
    delta = wrapped(grid - coord, period)
    value = jnp.exp(-0.5 * delta * delta * inv_var)
    return value, delta * inv_var * value


def iota(shape, dim):
    return lax.broadcasted_iota(jnp.int32, shape, dim)


def row_class(rows, members):
    share = rows // members
    bit = 0
    while (share << bit) % 8:
        bit += 1
    return share, bit, share << bit


def local_rows(shape, member, bit, block):
    row = iota(shape, 0)
    own = (member >> bit) & 1
    return ((row // block) * (2 * block) + own * block + row % block).astype(F32)


def prep_kernel(coords, par, spots, obs, weight, up, down, sem, *, thick, bit, half):
    own = (lax.axis_index("replica") >> bit) & 1
    block = obs.shape[3]
    copies = []
    for target, first in ((up, thick - HALO), (down, 0)):
        for n, source in enumerate((obs, weight)):
            for plane in range(HALO):
                for q in range(half // block):
                    row = (n * HALO + plane) * half + q * block
                    copies.append(
                        pltpu.make_async_copy(
                            source.at[first + plane, q, own],
                            target.at[pl.ds(row, block)],
                            sem.at[len(copies)],
                        )
                    )
                    copies[-1].start()
    data = jnp.concatenate([coords[...], par[1:2]], 0)
    high = data.astype(BF16)
    rest = data - high.astype(F32)
    mid = rest.astype(BF16)
    low = (rest - mid.astype(F32)).astype(BF16)
    pieces = jnp.concatenate([high.astype(F32), mid.astype(F32), low.astype(F32)], 0).astype(BF16)
    count = coords.shape[1]
    base = 2 * HALO * half
    for side, target in enumerate((up, down)):
        chosen = spots[side : side + 1, :]
        pick = (iota((count, chosen.shape[1]), 0) == chosen).astype(F32).astype(BF16)
        got = jnp.dot(pieces, pick, preferred_element_type=F32)
        got = got[0:4] + got[4:8] + got[8:12]
        groups = chosen.shape[1] // CELL
        for n in range(4):
            for g in range(groups):
                target[base + n * groups + g : base + n * groups + g + 1, :] = got[
                    n : n + 1, g * CELL : (g + 1) * CELL
                ]
    for copy in copies:
        copy.wait()


def spread_kernel(allc, par, out, up, down, left, *, thick, n_x, bit, block):
    members, _, count = allc.shape
    planes, half, depth = out.shape
    rows = 2 * half
    brick = lax.axis_index("brick")
    amp, inv_var = par[0:1], par[2:3]
    y_grid = local_rows((half, count), lax.axis_index("replica"), bit, block)
    z_grid = iota((depth, count), 0).astype(F32)
    x_grid = (iota((16, count), 0) + (brick * thick - HALO)).astype(F32)
    out[...] = jnp.zeros_like(out)

    def member(m, carry):
        place = allc[m]
        x_val, _ = gauss(x_grid, place[0:1], inv_var, n_x)
        y_val, _ = gauss(y_grid, place[1:2], inv_var, rows)
        z_val, _ = gauss(z_grid, place[2:3], inv_var, depth)
        x_amp = amp * x_val
        for i in range(planes):
            left[i * half : (i + 1) * half, :] = (x_amp[i : i + 1] * y_val).astype(BF16)
        got = lax.dot_general(left[...], z_val.astype(BF16), NT, preferred_element_type=F32)
        out[...] += got.reshape(planes, half, depth)
        return carry

    lax.fori_loop(0, members, member, 0)
    up[...] = out[thick:]
    down[...] = out[:RIM]


def pair_kernel(coords, par, low, high, lists, live, out, place_f, place_y, place_z, load, *, n_x, base):
    count = coords.shape[1]
    cells = count // CELL
    slabs = lax.axis_size("brick")
    brick = lax.axis_index("brick")
    scale = float(2**25)

    def fixed(v):
        whole = jnp.floor(v)
        return (whole.astype(jnp.int32) << 25) + ((v - whole) * scale).astype(jnp.int32)

    ghosts = (low.shape[0] - base) // 4
    shift_low = jnp.where(brick == 0, -float(n_x), 0.0).astype(F32)
    shift_high = jnp.where(brick == slabs - 1, float(n_x), 0.0).astype(F32)

    def column(row):
        return jnp.broadcast_to(row, (CELL, CELL)).T

    def enter(n, x, y, z, q):
        at = slice(n * CELL, (n + 1) * CELL)
        place_f[at, :] = column(x * scale)
        place_y[at, :] = column(fixed(y))
        place_z[at, :] = column(fixed(z))
        load[at, :] = column(q)

    for c in range(cells):
        at = slice(c * CELL, (c + 1) * CELL)
        enter(c, coords[0:1, at], coords[1:2, at], coords[2:3, at], par[1:2, at])
    for n, (ref, shift) in enumerate(((low, shift_low), (high, shift_high))):
        for g in range(ghosts):
            row = [ref[base + k * ghosts + g : base + k * ghosts + g + 1, :] for k in range(4)]
            enter(cells + n * ghosts + g, row[0] + shift, row[1], row[2], row[3])

    for c in range(cells):
        at = slice(c * CELL, (c + 1) * CELL)
        xi = jnp.broadcast_to(coords[0:1, at] * scale, (8, CELL))
        yi = jnp.broadcast_to(fixed(coords[1:2, at]), (8, CELL))
        zi = jnp.broadcast_to(fixed(coords[2:3, at]), (8, CELL))

        def slot(s, total):
            start = pl.multiple_of(lists[c, s] * CELL, CELL)
            tx, ty, tz = total
            for g in range(CELL // 8):
                here = pl.ds(start + g * 8, 8)
                dx = xi - place_f[here, :]
                dy = (yi - place_y[here, :]).astype(F32)
                dz = (zi - place_z[here, :]).astype(F32)
                dist = dx * dx + dy * dy + (dz * dz + softening * scale * scale)
                inv = lax.rsqrt(dist)
                w = load[here, :] * inv * (inv * inv)
                tx, ty, tz = tx + w * dx, ty + w * dy, tz + w * dz
            return tx, ty, tz

        zero = jnp.zeros((8, CELL), F32)
        total = lax.fori_loop(0, live[c], slot, (zero, zero, zero))
        factor = (coupling * scale * scale) * par[1:2, at]
        for k in range(3):
            out[k : k + 1, at] = factor * jnp.sum(total[k], axis=0, keepdims=True)


def force_kernel(
    allc, par, total, low, high, near_low, near_high, obs, weight,
    dev_out, own_out, partner_out,
    obs_s, weight_s, grad, dev_s, sem, *, thick, n_x, bit, share, members,
):
    planes, half, depth = total.shape
    count = allc.shape[2]
    rows = 2 * half
    block = obs.shape[3]
    member = lax.axis_index("replica")
    own = (member >> bit) & 1
    brick = lax.axis_index("brick")
    copies = []
    for n, (source, target) in enumerate(((obs, obs_s), (weight, weight_s))):
        for q in range(half // block):
            copies.append(
                pltpu.make_async_copy(
                    source.at[:, q, own],
                    target.at[pl.ds(HALO, thick), pl.ds(q * block, block)],
                    sem.at[len(copies)],
                )
            )
            copies[-1].start()
    for ref, first in ((near_low, 0), (near_high, thick + HALO)):
        for plane in range(HALO):
            obs_s[first + plane] = ref[plane * half : (plane + 1) * half, :]
            at = (HALO + plane) * half
            weight_s[first + plane] = ref[at : at + half, :]
    for copy in copies:
        copy.wait()
    for i in range(planes):
        summed = total[i]
        if i < RIM:
            summed = summed + low[i]
        if i >= thick:
            summed = summed + high[i - thick]
        dev = summed / members - obs_s[i]
        grad[i * half : (i + 1) * half, :] = (restraint * weight_s[i] * dev).astype(BF16)
        if HALO <= i < thick + HALO:
            dev_s[i - HALO] = dev
    first_row = member * share
    spot = (first_row // (2 * block)) * block + first_row % block
    for n in range(half // share):

        @pl.when(spot == n * share)
        def _(n=n):
            dev_out[...] = dev_s[:, n * share : (n + 1) * share, :]

    x_grid = (iota((16, CELL), 0) + (brick * thick - HALO)).astype(F32)
    y_grid = local_rows((half, CELL), member, bit, block)
    z_grid = iota((depth, CELL), 0).astype(F32)
    for out, m in ((own_out, member), (partner_out, member ^ (1 << bit))):
        for t in range(count // CELL):
            at = slice(t * CELL, (t + 1) * CELL)
            place = allc[m, :, at]
            inv_var = par[2:3, at]
            x_val, x_der = gauss(x_grid, place[0:1], inv_var, n_x)
            y_val, y_der = gauss(y_grid, place[1:2], inv_var, rows)
            z_val, z_der = gauss(z_grid, place[2:3], inv_var, depth)
            z_pair = jnp.concatenate([z_val, z_der], 1).astype(BF16)
            got = jnp.dot(grad[...], z_pair, preferred_element_type=F32)
            sums = [jnp.zeros((8, CELL), F32) for _ in range(3)]
            for i in range(planes):
                part = [jnp.zeros((8, CELL), F32) for _ in range(3)]
                for g in range(half // 8):
                    j = slice(g * 8, (g + 1) * 8)
                    k = slice(i * half + g * 8, i * half + (g + 1) * 8)
                    along, across = got[k, :CELL], got[k, CELL:]
                    part[0] += y_val[j] * along
                    part[1] += y_der[j] * along
                    part[2] += y_val[j] * across
                sums[0] += x_der[i : i + 1] * part[0]
                sums[1] += x_val[i : i + 1] * part[1]
                sums[2] += x_val[i : i + 1] * part[2]
            for k in range(3):
                out[k : k + 1, at] = -par[0:1, at] * jnp.sum(sums[k], axis=0, keepdims=True)


def local(
    atom_locations,
    atom_speeds_vector,
    inertial_amounts,
    electric_loads,
    scatter_strengths,
    gaussian_spreads_sigma,
    atom_present_flags,
    observed_volume_values,
    voxel_reciprocal_spread,
    paired_partner_lists,
    cell_usage_tally,
    halo_sender_spots,
    target_warmth_levels,
):
    thick, rows, depth = observed_volume_values.shape
    slabs = lax.axis_size("brick")
    members = lax.axis_size("replica")
    n_x = thick * slabs
    coords = atom_locations[0]
    count = coords.shape[1]
    planes = thick + 2 * HALO
    share, bit, block = row_class(rows, members)
    half = rows // 2
    base = 2 * HALO * half
    ghosts = halo_sender_spots.shape[1]
    near_rows = base + 4 * ghosts // CELL

    everyone = lax.all_to_all(
        jnp.broadcast_to(coords[None], (members,) + coords.shape), "replica", 0, 0
    )
    occupancy = atom_present_flags.astype(F32)
    par = jnp.stack(
        [
            occupancy * scatter_strengths,
            occupancy * electric_loads,
            1.0 / (gaussian_spreads_sigma * gaussian_spreads_sigma),
            inertial_amounts,
        ]
    )
    obs = observed_volume_values.reshape(thick, half // block, 2, block, depth)
    weight = voxel_reciprocal_spread.reshape(thick, half // block, 2, block, depth)
    near = jax.ShapeDtypeStruct((near_rows, CELL), F32)
    near_up, near_down = pl.pallas_call(
        functools.partial(prep_kernel, thick=thick, bit=bit, half=half),
        out_shape=(near, near),
        in_specs=[VMEM, VMEM, VMEM, ANY, ANY],
        out_specs=(VMEM, VMEM),
        scratch_shapes=[pltpu.SemaphoreType.DMA((4 * HALO * (half // block),))],
        name="prep",
    )(coords, par, halo_sender_spots, obs, weight)

    ring = [(i, (i + 1) % slabs) for i in range(slabs)]
    back = [(target, source) for source, target in ring]
    near_low = lax.ppermute(near_up, "brick", ring)
    near_high = lax.ppermute(near_down, "brick", back)

    rim = jax.ShapeDtypeStruct((RIM, half, depth), F32)
    total, rim_up, rim_down = pl.pallas_call(
        functools.partial(spread_kernel, thick=thick, n_x=n_x, bit=bit, block=block),
        out_shape=(jax.ShapeDtypeStruct((planes, half, depth), F32), rim, rim),
        in_specs=[VMEM, VMEM],
        out_specs=(VMEM, VMEM, VMEM),
        scratch_shapes=[pltpu.VMEM((planes * half, count), BF16)],
        name="spread",
    )(everyone, par)
    low = lax.ppermute(rim_up, "brick", ring)
    high = lax.ppermute(rim_down, "brick", back)

    blocks = count // CELL + 2 * ghosts // CELL
    short = pl.pallas_call(
        functools.partial(pair_kernel, n_x=n_x, base=base),
        out_shape=jax.ShapeDtypeStruct((3, count), F32),
        in_specs=[VMEM, VMEM, VMEM, VMEM, SMEM, SMEM],
        out_specs=VMEM,
        scratch_shapes=[
            pltpu.VMEM((blocks * CELL, CELL), F32),
            pltpu.VMEM((blocks * CELL, CELL), jnp.int32),
            pltpu.VMEM((blocks * CELL, CELL), jnp.int32),
            pltpu.VMEM((blocks * CELL, CELL), F32),
        ],
        cost_estimate=pl.CostEstimate(flops=40_000_000, bytes_accessed=400_000, transcendentals=0),
        name="pair",
    )(coords, par, near_low, near_high, paired_partner_lists, cell_usage_tally)

    force = jax.ShapeDtypeStruct((3, count), F32)
    deviation, own, partner = pl.pallas_call(
        functools.partial(
            force_kernel, thick=thick, n_x=n_x, bit=bit, share=share, members=members
        ),
        out_shape=(jax.ShapeDtypeStruct((thick, share, depth), F32), force, force),
        in_specs=[VMEM] * 7 + [ANY, ANY],
        out_specs=(VMEM, VMEM, VMEM),
        scratch_shapes=[
            pltpu.VMEM((planes, half, depth), F32),
            pltpu.VMEM((planes, half, depth), F32),
            pltpu.VMEM((planes * half, depth), BF16),
            pltpu.VMEM((thick, half, depth), F32),
            pltpu.SemaphoreType.DMA((2 * (half // block),)),
        ],
        name="force",
    )(everyone, par, total, low, high, near_low, near_high, obs, weight)

    swap = [(i, i ^ (1 << bit)) for i in range(members)]
    other = lax.ppermute(partner, "replica", swap)
    mass = par[3:4]
    v_half = atom_speeds_vector[0] + timestep * (own + other + short) / mass
    part = jnp.sum(mass * v_half * v_half).reshape(1, 1)
    kinetic = part
    if slabs <= 4:
        for step in range(1, slabs):
            route = [(i, (i + step) % slabs) for i in range(slabs)]
            kinetic = kinetic + lax.ppermute(part, "brick", route)
    else:
        kinetic = lax.psum(part, "brick")
    present_moment = kinetic / (3 * count * slabs * boltzmann) + 1e-06
    rescale_ratio = jnp.sqrt(
        1.0 + heat_bath_damping * (target_warmth_levels.astype(F32)[:, None] / present_moment - 1.0)
    )
    new_velocities = rescale_ratio * v_half
    new_positions = coords + timestep * new_velocities
    return (new_positions[None], new_velocities[None], deviation)


def solution(mesh):
    return jax.shard_map(
        local,
        mesh=mesh,
        in_specs=(
            P("replica", None, "brick"),
            P("replica", None, "brick"),
            P("brick"),
            P("brick"),
            P("brick"),
            P("brick"),
            P("brick"),
            P("brick", None, None),
            P("brick", None, None),
            P("brick", None),
            P("brick"),
            P(None, "brick"),
            P("replica"),
        ),
        out_specs=(
            P("replica", None, "brick"),
            P("replica", None, "brick"),
            P("brick", "replica", None),
        ),
        check_vma=False,
    )
```

time: 138 us -> 54.1 us (0.39)
  waiting for transfers between devices: 48.5 us -> 4.02 us
  other arithmetic: 30 us -> 1.96 us
  Pallas kernels: 0 us -> 20 us
  starting transfers between devices: 6.2 us -> 17.8 us
  between operations: 15.8 us -> 4.2 us
  local copies, waits for them, and re-layouts: 16.3 us -> 5.85 us
  matrix products: 10.4 us -> 0 us
  blocking collectives: 8 us -> 0 us
  loops' own time: 2.32 us -> 0 us
    psum x1 -> x0, waiting for transfers between devices: 45.7 us -> none  [local(): summed = lax.psum(local_map, 'replica')]
    pallas_call x0 -> x4, Pallas kernels: none -> 20 us  [the longest x1 7.31 us: local(): pl.pallas_call(functools.partial(spread_kernel, thick=thick, n_x=n_x, bit...]
    reduce_sum x43 -> x1, other arithmetic: 20.8 us -> 1.33 us  [local(): part = jnp.sum(mass * v_half * v_half).reshape(1, 1)]
    gather x18 -> x0, local copies, waits for them, and re-layouts: 12.2 us -> none  [the longest x14 8.02 us: slot(): partner = jnp.take(blocks, paired_partner_lists[:, index], axis=1)]
    dot_general x28 -> x0, matrix products: 10.4 us -> none  [the longest x14 7.01 us: spread_one_plane(): lax.dot_general(left, z_fac, (((1,), (1,)), ((), ())), preferred_element_...]
    psum x1 -> x0, blocking collectives: 8 us -> none  [local(): lax.psum(jnp.sum(inertial_amounts[None, :] * v_half * v_half), 'brick')]
    all_to_all x0 -> x1, starting transfers between devices: none -> 7.42 us  [local(): lax.all_to_all(jnp.broadcast_to(coords[None], (members,) + coords.shape),...]
    ppermute x6 -> x8, starting transfers between devices: 6.16 us -> 10.4 us  [the longest x3 5.45 us: local(): kinetic = kinetic + lax.ppermute(part, 'brick', route)]
  transfers between devices with their start and end apart: 7 -> 9, of which waited for: 3 -> 3; matrix products, arithmetic and copies ran while one was open for 28% -> 1% of each run, Pallas kernels for 0% -> 27%
where the time goes in v1:
time: 54.1 us; the launch traced here: 53.8 us
  Pallas kernels  20 us (37%)
  starting transfers between devices  17.8 us (33%)
  local copies, waits for them, and re-layouts  5.85 us (11%)
  between operations  4.2 us (8%)
  waiting for transfers between devices  4.02 us (7%)
  other arithmetic  1.96 us (4%)
    all_to_all x1, starting transfers between devices, local(): lax.all_to_all(jnp.broadcast_to(coords[None], (members,) + coords.shape),...  7.42 us
    pallas_call x1, Pallas kernels, local(): pl.pallas_call(functools.partial(spread_kernel, thick=thick, n_x=n_x, bit...  7.31 us
    ppermute x3, starting transfers between devices, local(): kinetic = kinetic + lax.ppermute(part, 'brick', route)  5.45 us
    pallas_call x1, Pallas kernels, local(): pl.pallas_call(functools.partial(force_kernel, thick=thick, n_x=n_x, bit=...  5.27 us
    unnamed x31, local copies, waits for them, and re-layouts  5.19 us
    pallas_call x1, Pallas kernels, local(): pl.pallas_call(functools.partial(pair_kernel, n_x=n_x, base=base), out_sh...  4.72 us
    ppermute x1, waiting for transfers between devices, local(): low = lax.ppermute(rim_up, 'brick', ring)  2.84 us
    pallas_call x1, Pallas kernels, local(): pl.pallas_call(functools.partial(prep_kernel, thick=thick, bit=bit, half=...  2.65 us
  transfers between devices with their start and end apart: 9, of which 3 were waited for; matrix products, arithmetic and copies ran while one was open for 1% of the time, Pallas kernels for 27%

profile of v1, /device:TPU:0, one launch (start us, length us, event | category | flops | bytes accessed | tf_op | source)
XLA Modules:
  0.0 53.8 jit_solution(842928975744314694)
XLA Ops:
  0.6 0.7 %copy.25 = f32[1,3,768]{2,1,0:T(4,128)S(1)} copy(f32[1,3,768]{2,0,1:T(1,128)} %param.13) | data formatting | bytes 18432
  1.3 0.6 %broadcast_in_dim.15 = f32[8,3,768]{2,1,0:T(4,128)} broadcast(f32[3,768]{1,0:T(4,128)S(1)} %bitcast.21), dimensions={1,2} | broadcast | bytes 82944 | tf_op jit(solution)/shard_map/broadcast_in_dim | solution.py:292
  2.0 0.0 copy-done.3
  2.0 7.4 %all-to-all-start = ((f32[8,3,768]{2,1,0:T(4,128)}), f32[8,3,768]{2,1,0:T(4,128)S(1)}, u32[]{:S(2)}, u32[]{:S(2)}) async-start(f32[8,3,768]{2,1,0:T(4,128)} %broadcast_in_dim.15), calls=%async_computation | async-start | bytes 196608 | tf_op jit(solution)/shard_map/all_to_all | solution.py:291
  9.4 0.0 copy-done.10
  9.4 0.0 copy-done.11
  9.4 0.0 copy-done.12
  9.4 0.0 copy-start.13
  9.5 0.7 %copy-done.13 = f32[768]{0:T(1024)S(1)} copy-done((f32[768]{0:T(1024)S(1)}, f32[768]{0:T(1024)}, u32[]{:S(2)}) %copy-start.13) | copy-done | bytes 3096
  10.1 0.0 copy-start.7
  10.2 0.7 %copy-done.7 = f32[768]{0:T(1024)S(1)} copy-done((f32[768]{0:T(1024)S(1)}, f32[768]{0:T(1024)}, u32[]{:S(2)}) %copy-start.7) | copy-done | bytes 3096
  10.8 0.6 %pad_maximum_fusion.par = f32[4,768]{1,0:T(4,128)} fusion(f32[1,768]{1,0:T(1,128)S(1)} %stack.18, f32[1,768]{1,0:T(1,128)S(1)} %stack.17, f32[1,768]{1,0:T(1,128)S(1)} %stack.16, f32[1,768]{1,0:T(1,128)S(1)} %stack.15), kind=kLoop, calls=%fused_computation.3 | loop fusion | flops 9216 | bytes 24576 | tf_op jit(solution)/shard_map/stack | solution.py:295
  11.5 2.7 %prep.1 = (f32[264,128]{1,0:T(8,128)}, f32[264,128]{1,0:T(8,128)}) custom-call(f32[3,768]{1,0:T(4,128)} %bitcast.22, f32[4,768]{1,0:T(4,128)} %pad_maximum_fusion.par, s32[2,256]{1,0:T(2,128)} %spots.1, f32[10,4,2,16,128]{4,3,2,1,0:T(8,128)} %bitcast.17, f32[10,4,2,16,128]{4,3,2,1,0:T(8,128)} %bitcast.19), custom_call_target="tpu_custom_call" | custom-call | tf_op jit(solution)/shard_map/prep/pallas_call | solution.py:306
  14.1 0.1 collective-permute-start.2
  14.2 1.7 %collective-permute-start.3 = (f32[264,128]{1,0:T(8,128)}, f32[264,128]{1,0:T(8,128)S(1)}, u32[]{:S(2)}, u32[]{:S(2)}) collective-permute-start(f32[264,128]{1,0:T(8,128)} %get-tuple-element.15), channel_id=1, source_target_pairs={{1,0},{2,1},{3,2},{0,3},{5,4},{6,5},{7,6},{4,7},{9,8},{10,9},{11,1... | collective-permute-start | bytes 405512 | tf_op jit(solution)/shard_map/ppermute | solution.py:318
  15.9 0.6 %all-to-all-done.allc = f32[8,3,768]{2,1,0:T(4,128)S(1)} async-done(((f32[8,3,768]{2,1,0:T(4,128)}), f32[8,3,768]{2,1,0:T(4,128)S(1)}, u32[]{:S(2)}, u32[]{:S(2)}) %all-to-all-start) | async-done | bytes 73760 | tf_op jit(solution)/shard_map/all_to_all | solution.py:291
  16.5 0.6 %copy-done = f32[8,3,768]{2,1,0:T(4,128)} copy-done((f32[8,3,768]{2,1,0:T(4,128)}, f32[8,3,768]{2,1,0:T(4,128)S(1)}, u32[]{:S(2)}) %copy-start) | copy-done | bytes 73752
  17.2 7.3 %spread.1 = (f32[14,64,128]{2,1,0:T(8,128)}, f32[4,64,128]{2,1,0:T(8,128)}, f32[4,64,128]{2,1,0:T(8,128)}) custom-call(f32[8,3,768]{2,1,0:T(4,128)} %copy-done, f32[4,768]{1,0:T(4,128)} %pad_maximum_fusion.par), custom_call_target="tpu_custom_call" | custom-call | tf_op jit(solution)/shard_map/spread/pallas_call | solution.py:321
  24.5 0.0 collective-permute-start
  24.5 1.7 %collective-permute-start.1 = (f32[4,64,128]{2,1,0:T(8,128)}, f32[4,64,128]{2,1,0:T(8,128)S(1)}, u32[]{:S(2)}, u32[]{:S(2)}) collective-permute-start(f32[4,64,128]{2,1,0:T(8,128)} %get-tuple-element.13), channel_id=1, source_target_pairs={{1,0},{2,1},{3,2},{0,3},{5,4},{6,5},{7,6},{4,7},{9,8},{10,9},{11,1... | collective-permute-start | bytes 393224 | tf_op jit(solution)/shard_map/ppermute | solution.py:330
  26.2 0.0 collective-permute-done.2.near_low.low
  26.2 0.0 collective-permute-done.3.near_high.high
  26.2 0.0 copy-start.2
  26.3 2.8 %collective-permute-done.low = f32[4,64,128]{2,1,0:T(8,128)S(1)} collective-permute-done((f32[4,64,128]{2,1,0:T(8,128)}, f32[4,64,128]{2,1,0:T(8,128)S(1)}, u32[]{:S(2)}, u32[]{:S(2)}) %collective-permute-start) | collective-permute-done | bytes 131104 | tf_op jit(solution)/shard_map/ppermute | solution.py:329
  29.1 0.5 collective-permute-done.1.high
  29.6 0.0 copy-done.1
  29.6 0.0 copy-done.2
  29.6 0.1 copy-done.4
  29.7 0.5 %copy-done.5 = f32[4,64,128]{2,1,0:T(8,128)} copy-done((f32[4,64,128]{2,1,0:T(8,128)}, f32[4,64,128]{2,1,0:T(8,128)S(1)}, u32[]{:S(2)}) %copy-start.5) | copy-done | bytes 131096
  30.3 5.3 %force.1 = (f32[10,16,128]{2,1,0:T(8,128)}, f32[3,768]{1,0:T(4,128)}, f32[3,768]{1,0:T(4,128)}) custom-call(f32[8,3,768]{2,1,0:T(4,128)} %copy-done, f32[4,768]{1,0:T(4,128)} %pad_maximum_fusion.par, f32[14,64,128]{2,1,0:T(8,128)} %get-tuple-element.11.total, f32[4,64,128]{2,1,0:T(8,128)} %copy-done.4, f32[4,64,128]{2,1,0:T(8,128)} %copy-done.5, ...), custom_call_target="tpu_custom_call" | custom-call | tf_op jit(solution)/shard_map/force/pallas_call | solution.py:349
  35.6 1.4 %collective-permute-start.4 = (f32[3,768]{1,0:T(4,128)}, f32[3,768]{1,0:T(4,128)S(1)}, u32[]{:S(2)}, u32[]{:S(2)}) collective-permute-start(f32[3,768]{1,0:T(4,128)} %get-tuple-element.17), channel_id=1, source_target_pairs={{0,4},{4,0},{8,12},{12,8},{16,20},{20,16},{24,28},{28,24},{1,5},{5... | collective-permute-start | bytes 27656 | tf_op jit(solution)/shard_map/ppermute | solution.py:367
  37.7 0.0 copy-start.8
  37.7 0.0 copy-start.9
  37.7 4.7 %pair.1 = f32[3,768]{1,0:T(4,128)} custom-call(f32[3,768]{1,0:T(4,128)} %bitcast.23, f32[4,768]{1,0:T(4,128)} %pad_maximum_fusion.par, f32[264,128]{1,0:T(8,128)} %copy-done.1, f32[264,128]{1,0:T(8,128)} %copy-done.2, s32[6,14]{1,0:T(8,128)} %lists.1, s32[6]{0:T(128)} %live.1), custom_call_target="tpu_custom_call" | custom-call | flops 40000000 | bytes 400000 | tf_op jit(solution)/shard_map/pair/pallas_call | solution.py:333
  42.4 0.0 collective-permute-done.4
  42.4 0.0 copy-done.8
  42.4 0.0 copy-done.9
  42.4 1.3 %fusion = (f32[]{:T(128)}, f32[3,768]{1,0:T(4,128)S(1)}) fusion(f32[768]{0:T(1024)S(1)} %copy-done.7, f32[3,768]{1,0:T(4,128)} %pair.1, f32[3,768]{1,0:T(4,128)S(1)} %copy-done.8, f32[3,768]{1,0:T(4,128)S(1)} %collective-permute-done.4, f32[1,3,768]{2,0,1:T(1,128)S(1)} %copy-done.9), kind=kLoop, calls=%fused_computation.2 | loop fusion | flops 18431 | bytes 49156 | tf_op jit(solution)/shard_map/reduce_sum | solution.py:370
  43.7 2.3 %collective-permute-start.5 = (f32[1,1]{1,0:T(1,128)}, f32[1,1]{1,0:T(1,128)}, u32[]{:S(2)}, u32[]{:S(2)}) collective-permute-start(f32[1,1]{1,0:T(1,128)} %bitcast.3), channel_id=1, source_target_pairs={{0,1},{1,2},{2,3},{3,0},{4,5},{5,6},{6,7},{7,4},{8,9},{9,10},{10,1... | collective-permute-start | bytes 20 | tf_op jit(solution)/shard_map/ppermute | solution.py:375
  46.0 1.7 %collective-permute-start.6 = (f32[1,1]{1,0:T(1,128)}, f32[1,1]{1,0:T(1,128)}, u32[]{:S(2)}, u32[]{:S(2)}) collective-permute-start(f32[1,1]{1,0:T(1,128)} %bitcast.3), channel_id=1, source_target_pairs={{0,2},{1,3},{2,0},{3,1},{4,6},{5,7},{6,4},{7,5},{8,10},{9,11},{10,... | collective-permute-start | bytes 20 | tf_op jit(solution)/shard_map/ppermute | solution.py:375
  47.7 1.5 %collective-permute-start.7 = (f32[1,1]{1,0:T(1,128)}, f32[1,1]{1,0:T(1,128)}, u32[]{:S(2)}, u32[]{:S(2)}) collective-permute-start(f32[1,1]{1,0:T(1,128)} %bitcast.3), channel_id=1, source_target_pairs={{0,3},{1,0},{2,1},{3,2},{4,7},{5,4},{6,5},{7,6},{8,11},{9,8},{10,9... | collective-permute-start | bytes 20 | tf_op jit(solution)/shard_map/ppermute | solution.py:375
  49.2 0.0 collective-permute-done.5
  50.6 0.0 collective-permute-done.6
  51.3 0.0 collective-permute-done.7
  51.9 0.0 copy-start.6
  52.0 0.6 %copy-done.6 = f32[1,3,768]{2,0,1:T(1,128)S(1)} copy-done((f32[1,3,768]{2,0,1:T(1,128)S(1)}, f32[1,3,768]{2,0,1:T(1,128)}, u32[]{:S(2)}) %copy-start.6) | copy-done | bytes 9240
  52.6 0.6 %copy.16 = f32[1,3,768]{2,0,1:T(1,128)} copy(f32[1,3,768]{2,1,0:T(4,128)S(1)} %get-tuple-element.25) | data formatting | bytes 18432
  53.2 0.6 %copy.17 = f32[1,3,768]{2,0,1:T(1,128)} copy(f32[1,3,768]{2,1,0:T(4,128)S(1)} %get-tuple-element.24) | data formatting | bytes 18432
  (15 shorter events, 0.0 us)
Async XLA Ops:
  1.3 0.6 %copy-start.3 = (f32[1,3,768]{2,1,0:T(4,128)}, f32[1,3,768]{2,1,0:T(4,128)S(1)}, u32[]{:S(2)}) copy-start(f32[1,3,768]{2,1,0:T(4,128)S(1)} %copy.25) | copy-start | bytes 27652
  2.0 7.4 %copy-start.10 = (f32[768]{0:T(1024)S(1)}, f32[768]{0:T(1024)}, u32[]{:S(2)}) copy-start(f32[768]{0:T(1024)} %param.17) | copy-start | bytes 9220
  2.0 7.4 %copy-start.11 = (s32[768]{0:T(1024)S(1)}, s32[768]{0:T(1024)}, u32[]{:S(2)}) copy-start(s32[768]{0:T(1024)} %param.19) | copy-start | bytes 9220
  2.0 7.4 %copy-start.12 = (f32[768]{0:T(1024)S(1)}, f32[768]{0:T(1024)}, u32[]{:S(2)}) copy-start(f32[768]{0:T(1024)} %param.16) | copy-start | bytes 9220
  2.0 14.5 %all-to-all-start = ((f32[8,3,768]{2,1,0:T(4,128)}), f32[8,3,768]{2,1,0:T(4,128)S(1)}, u32[]{:S(2)}, u32[]{:S(2)}) async-start(f32[8,3,768]{2,1,0:T(4,128)} %broadcast_in_dim.15), calls=%async_computation | async-start | bytes 196608 | tf_op jit(solution)/shard_map/all_to_all | solution.py:291
  9.4 0.7 %copy-start.13 = (f32[768]{0:T(1024)S(1)}, f32[768]{0:T(1024)}, u32[]{:S(2)}) copy-start(f32[768]{0:T(1024)} %param.18) | copy-start | bytes 9220
  10.1 0.7 %copy-start.7 = (f32[768]{0:T(1024)S(1)}, f32[768]{0:T(1024)}, u32[]{:S(2)}) copy-start(f32[768]{0:T(1024)} %param.15) | copy-start | bytes 9220
  14.1 12.1 %collective-permute-start.2 = (f32[264,128]{1,0:T(8,128)}, f32[264,128]{1,0:T(8,128)S(1)}, u32[]{:S(2)}, u32[]{:S(2)}) collective-permute-start(f32[264,128]{1,0:T(8,128)} %get-tuple-element.14), channel_id=1, source_target_pairs={{0,1},{1,2},{2,3},{3,0},{4,5},{5,6},{6,7},{7,4},{8,9},{9,10},{10,1... | collective-permute-start | bytes 405512 | tf_op jit(solution)/shard_map/ppermute | solution.py:317
  14.2 12.1 %collective-permute-start.3 = (f32[264,128]{1,0:T(8,128)}, f32[264,128]{1,0:T(8,128)S(1)}, u32[]{:S(2)}, u32[]{:S(2)}) collective-permute-start(f32[264,128]{1,0:T(8,128)} %get-tuple-element.15), channel_id=1, source_target_pairs={{1,0},{2,1},{3,2},{0,3},{5,4},{6,5},{7,6},{4,7},{9,8},{10,9},{11,1... | collective-permute-start | bytes 405512 | tf_op jit(solution)/shard_map/ppermute | solution.py:318
  16.5 0.6 %copy-start = (f32[8,3,768]{2,1,0:T(4,128)}, f32[8,3,768]{2,1,0:T(4,128)S(1)}, u32[]{:S(2)}) copy-start(f32[8,3,768]{2,1,0:T(4,128)S(1)} %all-to-all-done.allc) | copy-start | bytes 221188
  24.5 4.6 %collective-permute-start = (f32[4,64,128]{2,1,0:T(8,128)}, f32[4,64,128]{2,1,0:T(8,128)S(1)}, u32[]{:S(2)}, u32[]{:S(2)}) collective-permute-start(f32[4,64,128]{2,1,0:T(8,128)} %get-tuple-element.12), channel_id=1, source_target_pairs={{0,1},{1,2},{2,3},{3,0},{4,5},{5,6},{6,7},{7,4},{8,9},{9,10},{10,1... | collective-permute-start | bytes 393224 | tf_op jit(solution)/shard_map/ppermute | solution.py:329
  24.5 5.1 %collective-permute-start.1 = (f32[4,64,128]{2,1,0:T(8,128)}, f32[4,64,128]{2,1,0:T(8,128)S(1)}, u32[]{:S(2)}, u32[]{:S(2)}) collective-permute-start(f32[4,64,128]{2,1,0:T(8,128)} %get-tuple-element.13), channel_id=1, source_target_pairs={{1,0},{2,1},{3,2},{0,3},{5,4},{6,5},{7,6},{4,7},{9,8},{10,9},{11,1... | collective-permute-start | bytes 393224 | tf_op jit(solution)/shard_map/ppermute | solution.py:330
  26.2 3.4 %copy-start.1 = (f32[264,128]{1,0:T(8,128)}, f32[264,128]{1,0:T(8,128)S(1)}, u32[]{:S(2)}) copy-start(f32[264,128]{1,0:T(8,128)S(1)} %collective-permute-done.2.near_low.low) | copy-start | bytes 405508
  26.2 3.4 %copy-start.2 = (f32[264,128]{1,0:T(8,128)}, f32[264,128]{1,0:T(8,128)S(1)}, u32[]{:S(2)}) copy-start(f32[264,128]{1,0:T(8,128)S(1)} %collective-permute-done.3.near_high.high) | copy-start | bytes 405508
  29.1 0.7 %copy-start.4 = (f32[4,64,128]{2,1,0:T(8,128)}, f32[4,64,128]{2,1,0:T(8,128)S(1)}, u32[]{:S(2)}) copy-start(f32[4,64,128]{2,1,0:T(8,128)S(1)} %collective-permute-done.low) | copy-start | bytes 393220
  29.6 0.7 %copy-start.5 = (f32[4,64,128]{2,1,0:T(8,128)}, f32[4,64,128]{2,1,0:T(8,128)S(1)}, u32[]{:S(2)}) copy-start(f32[4,64,128]{2,1,0:T(8,128)S(1)} %collective-permute-done.1.high) | copy-start | bytes 393220
  35.6 6.8 %collective-permute-start.4 = (f32[3,768]{1,0:T(4,128)}, f32[3,768]{1,0:T(4,128)S(1)}, u32[]{:S(2)}, u32[]{:S(2)}) collective-permute-start(f32[3,768]{1,0:T(4,128)} %get-tuple-element.17), channel_id=1, source_target_pairs={{0,4},{4,0},{8,12},{12,8},{16,20},{20,16},{24,28},{28,24},{1,5},{5... | collective-permute-start | bytes 27656 | tf_op jit(solution)/shard_map/ppermute | solution.py:367
  37.7 4.7 %copy-start.8 = (f32[3,768]{1,0:T(4,128)S(1)}, f32[3,768]{1,0:T(4,128)}, u32[]{:S(2)}) copy-start(f32[3,768]{1,0:T(4,128)} %get-tuple-element.16) | copy-start | bytes 27652
  37.7 4.7 %copy-start.9 = (f32[1,3,768]{2,0,1:T(1,128)S(1)}, f32[1,3,768]{2,0,1:T(1,128)}, u32[]{:S(2)}) copy-start(f32[1,3,768]{2,0,1:T(1,128)} %param.14) | copy-start | bytes 27652
  43.7 5.5 %collective-permute-start.5 = (f32[1,1]{1,0:T(1,128)}, f32[1,1]{1,0:T(1,128)}, u32[]{:S(2)}, u32[]{:S(2)}) collective-permute-start(f32[1,1]{1,0:T(1,128)} %bitcast.3), channel_id=1, source_target_pairs={{0,1},{1,2},{2,3},{3,0},{4,5},{5,6},{6,7},{7,4},{8,9},{9,10},{10,1... | collective-permute-start | bytes 20 | tf_op jit(solution)/shard_map/ppermute | solution.py:375
  46.0 4.5 %collective-permute-start.6 = (f32[1,1]{1,0:T(1,128)}, f32[1,1]{1,0:T(1,128)}, u32[]{:S(2)}, u32[]{:S(2)}) collective-permute-start(f32[1,1]{1,0:T(1,128)} %bitcast.3), channel_id=1, source_target_pairs={{0,2},{1,3},{2,0},{3,1},{4,6},{5,7},{6,4},{7,5},{8,10},{9,11},{10,... | collective-permute-start | bytes 20 | tf_op jit(solution)/shard_map/ppermute | solution.py:375
  47.7 3.5 %collective-permute-start.7 = (f32[1,1]{1,0:T(1,128)}, f32[1,1]{1,0:T(1,128)}, u32[]{:S(2)}, u32[]{:S(2)}) collective-permute-start(f32[1,1]{1,0:T(1,128)} %bitcast.3), channel_id=1, source_target_pairs={{0,3},{1,0},{2,1},{3,2},{4,7},{5,4},{6,5},{7,6},{8,11},{9,8},{10,9... | collective-permute-start | bytes 20 | tf_op jit(solution)/shard_map/ppermute | solution.py:375
  51.9 0.7 %copy-start.6 = (f32[1,3,768]{2,0,1:T(1,128)S(1)}, f32[1,3,768]{2,0,1:T(1,128)}, u32[]{:S(2)}) copy-start(f32[1,3,768]{2,0,1:T(1,128)} %param.13) | copy-start | bytes 27652
